TPU v7x, 256 devices: a whole 4x4x8 slice. The times are simulated.
256 devices in a mesh: pop: 32 (over x, y, core), site: 8 (over z).
Axes of the slice: x: 4, y: 4, z: 8, core: 2. Of those that a mesh axis runs over, the one named last changes fastest.
Arguments:
- profile: bfloat16 [32768, 96], P(('pop', 'site')), may hold values from 0 to 1
- panel: bfloat16 [32768, 128], P(('pop', 'site')), may hold values from -6 to 6
- visit_person: int32 [131072], P(('pop', 'site')), may hold values from 0 to 127
- visit_owner: int32 [131072], P(('pop', 'site')), may hold values from 0 to 31, as said below
- visit_row: int32 [131072], P(('pop', 'site')), may hold values from 0 to 1023, as said below
- visit_start: int32 [131072], P(('pop', 'site')), may hold values from 0 to 95
- visit_length: int32 [131072], P(('pop', 'site')), may hold values from 2 to 48
- tile_loc: int32 [2048], P(('pop', 'site')), may hold values from 0 to 7
Outputs:
- exposure: bfloat16 [32768, 128], P(('pop', 'site'))
Inputs may be any that keep to these rules, and one draw needn't show every extreme that they name: `visit_owner`: all devices with one site index send the same number of visits to a given owner index; at most 24 visits of one device go to one owner index, and in every draw some owner index receives exactly 24 from every device of a site index. `visit_row`: among the visits that reach one owner device the rows are distinct; in each tile the rows that are used come first and the rest are empty.
All inputs are finite; a program needn't handle non-finite values.
Results may differ from a plain program's by a relative error of at most 0.013.
Values may be sent and summed in bfloat16 or wider, within the bound.
No kernel may reach another device: no remote copies, remote signals or barrier semaphores. Data moves between devices by JAX's collectives and lax.ppermute only.
A program may use at most 64 MiB of HBM per device.

v0:
```python
import math
import jax
import jax.numpy as jnp
from jax import lax
from jax.sharding import PartitionSpec as P


def pair_terms(own_weights, own_places, running, pieces):
    far_weights, far_panel, far_places = pieces
    piece_tiles = far_weights.shape[0]
    group_size = math.gcd(piece_tiles, 8)
    group_count = piece_tiles // group_size
    grouped = (
        far_weights.reshape((group_count, group_size) + far_weights.shape[1:]),
        far_panel.reshape((group_count, group_size) + far_panel.shape[1:]),
        far_places.reshape(group_count, group_size),
    )

    def one_group(carried, item):
        group_weights, group_panel, group_places = item
        same_place = (own_places[:, None] == group_places[None, :]).astype(jnp.bfloat16)
        masked_far = group_weights[None, :, :, :] * same_place[:, :, None, None]
        copresence = jnp.einsum(
            "ars,abqs->abrq", own_weights, masked_far, preferred_element_type=jnp.float32
        )
        high_part = copresence.astype(jnp.bfloat16)
        low_part = (copresence - high_part.astype(jnp.float32)).astype(jnp.bfloat16)
        added = jnp.einsum(
            "abrq,bqc->arc", high_part, group_panel, preferred_element_type=jnp.float32
        )
        added = added + jnp.einsum(
            "abrq,bqc->arc", low_part, group_panel, preferred_element_type=jnp.float32
        )
        return (carried + added, None)

    result_sum, unused = lax.scan(one_group, running, grouped)
    return result_sum


def per_device(
    profile, panel, visit_person, visit_owner, visit_row, visit_start, visit_length, tile_loc
):
    pop_count = lax.axis_size("pop")
    visit_count = visit_person.shape[0]
    person_count, slot_count = profile.shape
    panel_width = panel.shape[1]
    capacity = visit_count // pop_count * 3 // 2
    tile_count = tile_loc.shape[0]
    row_count = tile_count * 128
    slot_ids = jnp.arange(slot_count, dtype=jnp.int32)
    finish = jnp.minimum(visit_start + visit_length, slot_count)
    inside = (slot_ids[None, :] >= visit_start[:, None]) & (slot_ids[None, :] < finish[:, None])
    weights = jnp.where(inside, profile[visit_person], jnp.zeros((), jnp.bfloat16))
    visit_panel = panel[visit_person]
    owner_hot = (visit_owner[:, None] == jnp.arange(pop_count, dtype=jnp.int32)[None, :]).astype(
        jnp.int32
    )
    position = jnp.sum((jnp.cumsum(owner_hot, axis=0) - 1) * owner_hot, axis=1)
    send_index = visit_owner * capacity + position
    send_weights = (
        jnp.zeros((pop_count * capacity, slot_count), jnp.bfloat16)
        .at[send_index]
        .set(weights)
        .reshape(pop_count, capacity, slot_count)
    )
    send_panel = (
        jnp.zeros((pop_count * capacity, panel_width), jnp.bfloat16)
        .at[send_index]
        .set(visit_panel)
        .reshape(pop_count, capacity, panel_width)
    )
    send_rows = (
        jnp.full((pop_count * capacity,), row_count, jnp.int32)
        .at[send_index]
        .set(visit_row)
        .reshape(pop_count, capacity)
    )
    got_weights, got_panel, got_rows = (
        lax.all_to_all(send_weights, "pop", split_axis=0, concat_axis=0, tiled=True),
        lax.all_to_all(send_panel, "pop", split_axis=0, concat_axis=0, tiled=True),
        lax.all_to_all(send_rows, "pop", split_axis=0, concat_axis=0, tiled=True),
    )
    target = got_rows.reshape(-1)
    tile_weights = (
        jnp.zeros((row_count, slot_count), jnp.bfloat16)
        .at[target]
        .set(got_weights.reshape(-1, slot_count), mode="drop")
        .reshape(tile_count, 128, slot_count)
    )
    tile_panel = (
        jnp.zeros((row_count, panel_width), jnp.bfloat16)
        .at[target]
        .set(got_panel.reshape(-1, panel_width), mode="drop")
        .reshape(tile_count, 128, panel_width)
    )
    initial = jnp.zeros((tile_count, 128, panel_width), jnp.float32)
    summed_rows = pair_terms(
        tile_weights,
        tile_loc,
        initial,
        (
            lax.all_gather(tile_weights, "site", axis=0, tiled=True),
            lax.all_gather(tile_panel, "site", axis=0, tiled=True),
            lax.all_gather(tile_loc, "site", axis=0, tiled=True),
        ),
    )
    row_result = (summed_rows / slot_count).astype(jnp.bfloat16).reshape(row_count, panel_width)
    sent_back = row_result[jnp.minimum(got_rows, row_count - 1)]
    returned = lax.all_to_all(sent_back, "pop", split_axis=0, concat_axis=0, tiled=True)
    own_results = returned.reshape(pop_count * capacity, panel_width)[send_index]
    person_hot = (
        jnp.arange(person_count, dtype=jnp.int32)[:, None] == visit_person[None, :]
    ).astype(jnp.bfloat16)
    return jnp.dot(person_hot, own_results, preferred_element_type=jnp.float32).astype(jnp.bfloat16)


def solution(mesh):
    placed = (
        P(("pop", "site"), None),
        P(("pop", "site"), None),
        P(("pop", "site")),
        P(("pop", "site")),
        P(("pop", "site")),
        P(("pop", "site")),
        P(("pop", "site")),
        P(("pop", "site")),
    )
    return jax.shard_map(
        per_device, mesh=mesh, in_specs=placed, out_specs=P(("pop", "site"), None), check_vma=False
    )
```

profile of v0, /device:TPU:1, one launch (start us, length us, event | category | flops | bytes accessed | tf_op | source)
XLA Modules:
  0.0 205.3 jit_solution(10561987336551839992)
XLA Ops:
  10.2 2.6 %scatter_custom_fusion = s32[768]{0:T(1024)S(1)} fusion(s32[512]{0:T(512)S(1)} %get-tuple-element.104, s32[512]{0:T(512)} %param.14, s32[]{:T(128)} %constant.8.clone.1), kind=kCustom, calls=%fused_computation.71 | custom fusion | bytes 3584 | tf_op jit(solution)/shard_map/scatter | solution.py:75
  13.5 8.6 %all-to-all-start = ((s32[32,1,24]{2,1,0:T(1,128)}), s32[32,1,24]{2,1,0:T(1,128)S(1)}, u32[]{:S(2)}, u32[]{:S(2)}) async-start(s32[32,1,24]{2,1,0:T(1,128)} %bitcast.2), calls=%async_computation | async-start | bytes 32768 | tf_op jit(solution)/shard_map/all_to_all | solution.py:81
  23.6 3.9 %scatter_custom_fusion.1 = bf16[768,96]{1,0:T(8,128)(2,1)} fusion(s32[512]{0:T(512)S(1)} %get-tuple-element.104, s32[512]{0:T(512)S(1)} %get-tuple-element.105, s32[512]{0:T(512)} %param.15, bf16[]{:T(256)} %constant.19.clone.1, bf16[128,96]{1,0:T(8,128)(2,1)S(1)} %copy.29, s32[1024]{0:T(1024)S(1)} %pad_clamp_fusion.2), kind=kCustom, calls=%fused_computation.40 | custom fusion | flops 196608 | bytes 189440 | tf_op jit(solution)/shard_map/scatter | solution.py:63
  28.9 6.0 %all-to-all-start.1 = ((bf16[32,24,96]{2,1,0:T(8,128)(2,1)}), bf16[32,24,96]{2,1,0:T(8,128)(2,1)S(1)}, u32[]{:S(2)}, u32[]{:S(2)}) async-start(bf16[32,24,96]{2,1,0:T(8,128)(2,1)} %bitcast.3), calls=%async_computation.1 | async-start | bytes 393216 | tf_op jit(solution)/shard_map/all_to_all | solution.py:79
  36.3 7.0 %all-to-all-done.1 = bf16[32,24,96]{2,1,0:T(8,128)(2,1)S(1)} async-done(((bf16[32,24,96]{2,1,0:T(8,128)(2,1)}), bf16[32,24,96]{2,1,0:T(8,128)(2,1)S(1)}, u32[]{:S(2)}, u32[]{:S(2)}) %all-to-all-start.1) | async-done | bytes 147488 | tf_op jit(solution)/shard_map/all_to_all | solution.py:79
  43.2 4.3 %scatter_custom_fusion.2 = bf16[1024,96]{1,0:T(8,128)(2,1)S(1)} fusion(s32[768]{0:T(1024)S(1)} %fusion.39, bf16[768,96]{1,0:T(8,128)(2,1)S(1)} %bitcast.114, bf16[]{:T(256)} %constant.19.clone.1), kind=kCustom, calls=%fused_computation.47 | custom fusion | bytes 196610 | tf_op jit(solution)/shard_map/scatter | solution.py:87
  48.5 3.0 %scatter_custom_fusion.3 = bf16[768,128]{1,0:T(8,128)(2,1)S(1)} fusion(s32[512]{0:T(512)S(1)} %get-tuple-element.104, bf16[128,128]{1,0:T(8,128)(2,1)S(1)} %copy-done, s32[1024]{0:T(1024)S(1)} %pad_clamp_fusion.2, bf16[]{:T(256)} %constant.19.clone.1), kind=kCustom, calls=%fused_computation.41 | custom fusion | bytes 196610 | tf_op jit(solution)/shard_map/scatter | solution.py:69
  51.5 11.9 %all_to_all.24 = bf16[32,24,128]{2,1,0:T(8,128)(2,1)S(1)} all-to-all(bf16[32,24,128]{2,1,0:T(8,128)(2,1)S(1)} %bitcast.112), channel_id=1, replica_groups=mesh['pop'=32,'site'=8] {'pop'}, dimensions={0} | all-to-all | bytes 393216 | tf_op jit(solution)/shard_map/all_to_all | solution.py:80
  63.4 4.9 %scatter_custom_fusion.4 = bf16[1024,128]{1,0:T(8,128)(2,1)} fusion(s32[768]{0:T(1024)S(1)} %fusion.39, bf16[768,128]{1,0:T(8,128)(2,1)S(1)} %bitcast.115, bf16[]{:T(256)} %constant.19.clone.1), kind=kCustom, calls=%fused_computation.43 | custom fusion | bytes 262146 | tf_op jit(solution)/shard_map/scatter | solution.py:93
  69.9 13.6 %all-reduce = s32[64]{0:T(128)S(1)} all-reduce(s32[64]{0:T(128)S(1)} %dynamic-update-slice), channel_id=1, replica_groups=mesh['pop'=32,'site'=8] {'site'}, use_global_device_ids=true, to_apply=%add | all-reduce | flops 64 | bytes 512
  83.9 3.5 %all-gather.3.cloned.1.call-done = bf16[64,128,96]{1,0,2:T(8,128)(2,1)} async-done(((bf16[8,128,96]{1,0,2:T(8,128)(2,1)}), bf16[64,128,96]{1,0,2:T(8,128)(2,1)}) %all-gather.3.cloned.1.call-update) | async-done | bytes 1572880 | tf_op jit(solution)/shard_map/all_gather | solution.py:102
  87.3 42.4 %all-gather.5.cloned.1.call-done = bf16[64,128,128]{2,1,0:T(8,128)(2,1)} async-done(((bf16[8,128,128]{2,1,0:T(8,128)(2,1)}), bf16[64,128,128]{2,1,0:T(8,128)(2,1)}) %all-gather.5.cloned.1.call-update) | async-done | bytes 2097168 | tf_op jit(solution)/shard_map/all_gather | solution.py:103
  129.7 44.4 %while.11 = (s32[]{:T(128)}, f32[8,128,128]{2,1,0:T(8,128)S(1)}, bf16[8,8,128,96]{2,1,0,3:T(8,128)(2,1)}, s32[8]{0:T(128)S(1)}, s32[8,8]{1,0:T(8,128)S(1)}, /*in...) while((s32[]{:T(128)}, f32[8,128,128]{2,1,0:T(8,128)S(1)}, ...), condition=%wide.region_9.10_spmd.clone, body=%wide.region_8.9_spmd.clone.sunk | while | flops 743571584 | bytes 16384511 | solution.py:36
  131.7 1.7 fusion.67
  133.4 1.9 fusion.68
  137.3 1.7 fusion.67
  139.0 1.9 fusion.68
  142.8 1.7 fusion.67
  144.5 1.9 fusion.68
  148.4 1.7 fusion.67
  150.1 1.9 fusion.68
  153.9 1.7 fusion.67
  155.6 1.9 fusion.68
  159.5 1.7 fusion.67
  161.2 1.9 fusion.68
  165.0 1.7 fusion.67
  166.7 1.9 fusion.68
  170.6 1.7 fusion.67
  172.3 1.9 fusion.68
  174.3 2.5 %gather_fusion = bf16[768,128]{1,0:T(8,128)(2,1)} fusion(bf16[1024,128]{1,0:T(8,128)(2,1)S(1)} %bitcast.106, s32[1024]{0:T(1024)S(1)} %pad_clamp_fusion.1), kind=kCustom, calls=%fused_computation.2 | custom fusion | bytes 396288 | tf_op jit(solution)/shard_map/gather | solution.py:108
  176.8 11.2 %all-to-all-start.3 = ((bf16[32,24,128]{2,1,0:T(8,128)(2,1)}), bf16[32,24,128]{2,1,0:T(8,128)(2,1)S(1)}, u32[]{:S(2)}, u32[]{:S(2)}) async-start(bf16[32,24,128]{2,1,0:T(8,128)(2,1)} %bitcast.14), calls=%async_computation.3 | async-start | bytes 393216 | tf_op jit(solution)/shard_map/all_to_all | solution.py:109
  188.0 8.3 %all-to-all-done.3 = bf16[32,24,128]{2,1,0:T(8,128)(2,1)S(1)} async-done(((bf16[32,24,128]{2,1,0:T(8,128)(2,1)}), bf16[32,24,128]{2,1,0:T(8,128)(2,1)S(1)}, u32[]{:S(2)}, u32[]{:S(2)}) %all-to-all-start.3) | async-done | bytes 196640 | tf_op jit(solution)/shard_map/all_to_all | solution.py:109
  (82 shorter events, 28.6 us)
Async XLA Ops:
  6.5 41.9 %copy-start = (bf16[128,128]{1,0:T(8,128)(2,1)S(1)}, bf16[128,128]{1,0:T(8,128)(2,1)}, u32[]{:S(2)}) copy-start(bf16[128,128]{1,0:T(8,128)(2,1)} %param.11) | copy-start | bytes 98308
  6.5 61.8 %copy-start.3 = (u32[256]{0:T(256)S(1)}, u32[256]{0:T(256)}, u32[]{:S(2)}) copy-start(u32[256]{0:T(256)} %constant.52) | copy-start | bytes 3076
  6.5 63.1 %copy-start.1 = (s32[8]{0:T(128)S(1)}, s32[8]{0:T(128)}, u32[]{:S(2)}) copy-start(s32[8]{0:T(128)} %param.17) | copy-start | bytes 100
  13.5 15.5 %all-to-all-start = ((s32[32,1,24]{2,1,0:T(1,128)}), s32[32,1,24]{2,1,0:T(1,128)S(1)}, u32[]{:S(2)}, u32[]{:S(2)}) async-start(s32[32,1,24]{2,1,0:T(1,128)} %bitcast.2), calls=%async_computation | async-start | bytes 32768 | tf_op jit(solution)/shard_map/all_to_all | solution.py:81
  28.9 14.3 %all-to-all-start.1 = ((bf16[32,24,96]{2,1,0:T(8,128)(2,1)}), bf16[32,24,96]{2,1,0:T(8,128)(2,1)S(1)}, u32[]{:S(2)}, u32[]{:S(2)}) async-start(bf16[32,24,96]{2,1,0:T(8,128)(2,1)} %bitcast.3), calls=%async_computation.1 | async-start | bytes 393216 | tf_op jit(solution)/shard_map/all_to_all | solution.py:79
  34.9 52.4 %all-gather.3.cloned.1.call-start = ((), (), s32[]{:S(2)}) async-start(), calls=%async_computation.4 | async-start | bytes 1769472 | tf_op jit(solution)/shard_map/all_gather | solution.py:102
  48.4 81.3 %all-gather.5.cloned.1.call-start = ((), (), s32[]{:S(2)}) async-start(), calls=%async_computation.5 | async-start | bytes 2359296 | tf_op jit(solution)/shard_map/all_gather | solution.py:103
  174.2 23.5 %copy-start.2 = (s32[512]{0:T(512)S(1)}, s32[512]{0:T(512)}, u32[]{:S(2)}) copy-start(s32[512]{0:T(512)} %param.12) | copy-start | bytes 6148
  176.8 19.6 %all-to-all-start.3 = ((bf16[32,24,128]{2,1,0:T(8,128)(2,1)}), bf16[32,24,128]{2,1,0:T(8,128)(2,1)S(1)}, u32[]{:S(2)}, u32[]{:S(2)}) async-start(bf16[32,24,128]{2,1,0:T(8,128)(2,1)} %bitcast.14), calls=%async_computation.3 | async-start | bytes 393216 | tf_op jit(solution)/shard_map/all_to_all | solution.py:109
Sparse Core Ops, SparseCore 0:
  48.5 38.7 all-gather.2
  89.1 40.5 all-gather.4
where the time goes:
time: 207 us; the launch traced here: 205 us
  waiting for transfers between devices  62.6 us (30%)
  matrix products  36.5 us (18%)
  local copies, waits for them, and re-layouts  30.9 us (15%)
  starting transfers between devices  25.9 us (13%)
  blocking collectives  25.5 us (12%)
  between operations  14.2 us (7%)
  other arithmetic  9.37 us (5%)
    all_gather x1, waiting for transfers between devices, per_device(): lax.all_gather(tile_panel, 'site', axis=0, tiled=True)  42.4 us
    dot_general x8, matrix products, one_group(): jnp.einsum('abrq,bqc->arc', high_part, group_panel, preferred_element_typ...  14.8 us
    unnamed x1, blocking collectives  13.6 us
    dot_general x8, matrix products, one_group(): jnp.einsum('abrq,bqc->arc', low_part, group_panel, preferred_element_type...  13.6 us
    all_to_all x1, blocking collectives, per_device(): lax.all_to_all(send_panel, 'pop', split_axis=0, concat_axis=0, tiled=True)  11.9 us
    all_to_all x1, starting transfers between devices, per_device(): lax.all_to_all(sent_back, 'pop', split_axis=0, concat_axis=0, tiled=True)  11.2 us
    all_to_all x1, starting transfers between devices, per_device(): lax.all_to_all(send_rows, 'pop', split_axis=0, concat_axis=0, tiled=True)  8.59 us
    all_to_all x1, waiting for transfers between devices, per_device(): lax.all_to_all(sent_back, 'pop', split_axis=0, concat_axis=0, tiled=True)  8.32 us
  transfers between devices with their start and end apart: 5, of which 5 were waited for; matrix products, arithmetic and copies ran while one was open for 8% of the time, Pallas kernels for 0%

commit v1 on v0

--- a/solution.py
+++ b/solution.py
@@ -3,6 +3,12 @@
 import jax.numpy as jnp
 from jax import lax
 from jax.sharding import PartitionSpec as P
+
+
+def point_islands(w_in):
+    return jnp.concatenate(
+        lax.all_to_all(jnp.stack(lax.axis_size("site") * [w_in]), "site", 0, 0), axis=0
+    )
 
 
 def pair_terms(own_weights, own_places, running, pieces):
@@ -100,7 +106,7 @@
         initial,
         (
             lax.all_gather(tile_weights, "site", axis=0, tiled=True),
-            lax.all_gather(tile_panel, "site", axis=0, tiled=True),
+            point_islands(tile_panel),
             lax.all_gather(tile_loc, "site", axis=0, tiled=True),
         ),
     )

time: 207 us -> 192 us (0.928)
  waiting for transfers between devices: 62.6 us -> 27 us
  blocking collectives: 25.5 us -> 53.4 us
  matrix products: 36.5 us -> 21.2 us
  starting transfers between devices: 25.9 us -> 32.4 us
    all_gather x1 -> x0, waiting for transfers between devices: 42.4 us -> none  [per_device(): lax.all_gather(tile_panel, 'site', axis=0, tiled=True)]
    unnamed x1, blocking collectives: 13.6 us -> 53.4 us
    all_to_all x0 -> x2, starting transfers between devices: none -> 13.2 us  [the longest x1 8.32 us: point_islands(): lax.all_to_all(jnp.stack(lax.axis_size('site') * [w_in]), 'site', 0, 0)]
    all_to_all x1 -> x0, blocking collectives: 11.9 us -> none  [per_device(): lax.all_to_all(send_panel, 'pop', split_axis=0, concat_axis=0, tiled=True)]
    dot_general x8, matrix products: 13.6 us -> 6.01 us  [one_group(): jnp.einsum('abrq,bqc->arc', low_part, group_panel, preferred_element_type...]
    dot_general x8, matrix products: 14.8 us -> 7.2 us  [one_group(): jnp.einsum('abrq,bqc->arc', high_part, group_panel, preferred_element_typ...]
    all_gather x1, waiting for transfers between devices: 3.46 us -> 9.78 us  [per_device(): lax.all_gather(tile_weights, 'site', axis=0, tiled=True)]
    all_to_all x1, starting transfers between devices: 11.2 us -> 6.65 us  [per_device(): lax.all_to_all(sent_back, 'pop', split_axis=0, concat_axis=0, tiled=True)]
  transfers between devices with their start and end apart: 5 -> 6, of which waited for: 5 -> 5; matrix products, arithmetic and copies ran while one was open for 8% -> 11% of each run, Pallas kernels for 0% -> 0%
where the time goes in v1:
time: 192 us; the launch traced here: 191 us
  blocking collectives  53.4 us (28%)
  local copies, waits for them, and re-layouts  32.8 us (17%)
  starting transfers between devices  32.4 us (17%)
  waiting for transfers between devices  27 us (14%)
  matrix products  21.2 us (11%)
  between operations  14.2 us (7%)
  other arithmetic  9.37 us (5%)
    unnamed x1, blocking collectives  53.4 us
    all_gather x1, waiting for transfers between devices, per_device(): lax.all_gather(tile_weights, 'site', axis=0, tiled=True)  9.78 us
    all_to_all x1, starting transfers between devices, per_device(): lax.all_to_all(send_rows, 'pop', split_axis=0, concat_axis=0, tiled=True)  8.59 us
    all_to_all x1, starting transfers between devices, point_islands(): lax.all_to_all(jnp.stack(lax.axis_size('site') * [w_in]), 'site', 0, 0)  8.32 us
    all_to_all x1, waiting for transfers between devices, per_device(): lax.all_to_all(sent_back, 'pop', split_axis=0, concat_axis=0, tiled=True)  8.32 us
    dynamic_slice x16, local copies, waits for them, and re-layouts, pair_terms(): result_sum, unused = lax.scan(one_group, running, grouped)  7.75 us
    dot_general x8, matrix products, one_group(): jnp.einsum('ars,abqs->abrq', own_weights, masked_far, preferred_element_t...  7.23 us
    dot_general x8, matrix products, one_group(): jnp.einsum('abrq,bqc->arc', high_part, group_panel, preferred_element_typ...  7.2 us
  transfers between devices with their start and end apart: 6, of which 5 were waited for; matrix products, arithmetic and copies ran while one was open for 11% of the time, Pallas kernels for 0%

profile of v1, /device:TPU:1, one launch (start us, length us, event | category | flops | bytes accessed | tf_op | source)
XLA Modules:
  0.0 190.8 jit_solution(9617595420994793594)
XLA Ops:
  7.2 1.2 reduce-window.6
  10.2 2.6 %scatter_custom_fusion = s32[768]{0:T(1024)S(1)} fusion(s32[512]{0:T(512)S(1)} %get-tuple-element.104, s32[512]{0:T(512)} %param.14, s32[]{:T(128)} %constant.8.clone.1), kind=kCustom, calls=%fused_computation.71 | custom fusion | bytes 3584 | tf_op jit(solution)/shard_map/scatter | solution.py:81
  13.5 8.6 %all-to-all-start = ((s32[32,1,24]{2,1,0:T(1,128)}), s32[32,1,24]{2,1,0:T(1,128)S(1)}, u32[]{:S(2)}, u32[]{:S(2)}) async-start(s32[32,1,24]{2,1,0:T(1,128)} %bitcast.2), calls=%async_computation | async-start | bytes 32768 | tf_op jit(solution)/shard_map/all_to_all | solution.py:87
  22.8 3.6 %scatter_custom_fusion.3 = bf16[768,128]{1,0:T(8,128)(2,1)} fusion(s32[512]{0:T(512)S(1)} %get-tuple-element.104, bf16[128,128]{1,0:T(8,128)(2,1)S(1)} %copy-done, s32[1024]{0:T(1024)S(1)} %pad_clamp_fusion.2, bf16[]{:T(256)} %constant.19.clone.1), kind=kCustom, calls=%fused_computation.41 | custom fusion | bytes 196610 | tf_op jit(solution)/shard_map/scatter | solution.py:75
  26.4 2.5 %all-to-all-done = s32[32,1,24]{2,1,0:T(1,128)S(1)} async-done(((s32[32,1,24]{2,1,0:T(1,128)}), s32[32,1,24]{2,1,0:T(1,128)S(1)}, u32[]{:S(2)}, u32[]{:S(2)}) %all-to-all-start) | async-done | bytes 3104 | tf_op jit(solution)/shard_map/all_to_all | solution.py:87
  28.9 4.8 %all-to-all-start.2 = ((bf16[32,24,128]{2,1,0:T(8,128)(2,1)}), bf16[32,24,128]{2,1,0:T(8,128)(2,1)S(1)}, u32[]{:S(2)}, u32[]{:S(2)}) async-start(bf16[32,24,128]{2,1,0:T(8,128)(2,1)} %bitcast.8), calls=%async_computation.2 | async-start | bytes 393216 | tf_op jit(solution)/shard_map/all_to_all | solution.py:86
  34.6 3.9 %scatter_custom_fusion.1 = bf16[768,96]{1,0:T(8,128)(2,1)} fusion(s32[512]{0:T(512)S(1)} %get-tuple-element.104, s32[512]{0:T(512)S(1)} %get-tuple-element.105, s32[512]{0:T(512)} %param.15, bf16[]{:T(256)} %constant.19.clone.1, bf16[128,96]{1,0:T(8,128)(2,1)S(1)} %copy.29, s32[1024]{0:T(1024)S(1)} %pad_clamp_fusion.2), kind=kCustom, calls=%fused_computation.40 | custom fusion | flops 196608 | bytes 189440 | tf_op jit(solution)/shard_map/scatter | solution.py:69
  38.5 3.6 %all-to-all-done.2 = bf16[32,24,128]{2,1,0:T(8,128)(2,1)S(1)} async-done(((bf16[32,24,128]{2,1,0:T(8,128)(2,1)}), bf16[32,24,128]{2,1,0:T(8,128)(2,1)S(1)}, u32[]{:S(2)}, u32[]{:S(2)}) %all-to-all-start.2) | async-done | bytes 196640 | tf_op jit(solution)/shard_map/all_to_all | solution.py:86
  42.1 3.8 %all-to-all-start.1 = ((bf16[32,24,96]{2,1,0:T(8,128)(2,1)}), bf16[32,24,96]{2,1,0:T(8,128)(2,1)S(1)}, u32[]{:S(2)}, u32[]{:S(2)}) async-start(bf16[32,24,96]{2,1,0:T(8,128)(2,1)} %bitcast.3), calls=%async_computation.1 | async-start | bytes 393216 | tf_op jit(solution)/shard_map/all_to_all | solution.py:85
  47.3 4.3 %scatter_custom_fusion.4 = bf16[1024,128]{1,0:T(8,128)(2,1)S(1)} fusion(s32[768]{0:T(1024)S(1)} %fusion.39, bf16[768,128]{1,0:T(8,128)(2,1)S(1)} %bitcast.112, bf16[]{:T(256)} %constant.19.clone.1), kind=kCustom, calls=%fused_computation.43 | custom fusion | bytes 262146 | tf_op jit(solution)/shard_map/scatter | solution.py:99
  51.6 2.8 %all-to-all-done.1 = bf16[32,24,96]{2,1,0:T(8,128)(2,1)S(1)} async-done(((bf16[32,24,96]{2,1,0:T(8,128)(2,1)}), bf16[32,24,96]{2,1,0:T(8,128)(2,1)S(1)}, u32[]{:S(2)}, u32[]{:S(2)}) %all-to-all-start.1) | async-done | bytes 147488 | tf_op jit(solution)/shard_map/all_to_all | solution.py:85
  54.3 1.9 stack.3
  56.2 8.3 %all-to-all-start.3 = ((bf16[8,8,128,128]{3,2,1,0:T(8,128)(2,1)}), bf16[8,8,128,128]{3,2,1,0:T(8,128)(2,1)S(1)}, u32[]{:S(2)}, u32[]{:S(2)}) async-start(bf16[8,8,128,128]{3,2,1,0:T(8,128)(2,1)} %stack.3), calls=%async_computation.3 | async-start | bytes 4194304 | tf_op jit(solution)/shard_map/all_to_all | solution.py:10
  64.8 4.3 %scatter_custom_fusion.2 = bf16[1024,96]{1,0:T(8,128)(2,1)S(1)} fusion(s32[768]{0:T(1024)S(1)} %fusion.39, bf16[768,96]{1,0:T(8,128)(2,1)S(1)} %bitcast.111, bf16[]{:T(256)} %constant.19.clone.1), kind=kCustom, calls=%fused_computation.47 | custom fusion | bytes 196610 | tf_op jit(solution)/shard_map/scatter | solution.py:93
  71.5 53.4 %all-reduce = s32[64]{0:T(128)S(1)} all-reduce(s32[64]{0:T(128)S(1)} %dynamic-update-slice), channel_id=1, replica_groups=mesh['pop'=32,'site'=8] {'site'}, use_global_device_ids=true, to_apply=%add | all-reduce | flops 64 | bytes 512
  125.2 9.8 %all-gather.2.cloned.1.call-done = bf16[64,128,96]{1,0,2:T(8,128)(2,1)} async-done(((bf16[8,128,96]{1,0,2:T(8,128)(2,1)}), bf16[64,128,96]{1,0,2:T(8,128)(2,1)}) %all-gather.2.cloned.1.call-update) | async-done | bytes 1572880 | tf_op jit(solution)/shard_map/all_gather | solution.py:108
  135.0 29.2 %while.11 = (s32[]{:T(128)}, f32[8,128,128]{2,1,0:T(8,128)S(1)}, bf16[8,8,128,96]{2,1,0,3:T(8,128)(2,1)}, s32[8]{0:T(128)S(1)}, s32[8,8]{1,0:T(8,128)S(1)}, /*in...) while((s32[]{:T(128)}, f32[8,128,128]{2,1,0:T(8,128)S(1)}, ...), condition=%wide.region_9.10_spmd.clone, body=%wide.region_8.9_spmd.clone.sunk | while | flops 743571584 | bytes 16384511 | solution.py:42
  135.1 0.9 constant_dynamic-slice_fusion.3
  136.1 0.9 fusion.66
  138.8 0.9 constant_dynamic-slice_fusion.3
  139.7 0.9 fusion.66
  142.4 0.9 constant_dynamic-slice_fusion.3
  143.4 0.9 fusion.66
  146.1 0.9 constant_dynamic-slice_fusion.3
  149.7 0.9 constant_dynamic-slice_fusion.3
  153.4 0.9 constant_dynamic-slice_fusion.3
  157.0 0.9 constant_dynamic-slice_fusion.3
  160.7 0.9 constant_dynamic-slice_fusion.3
  164.3 2.5 %gather_fusion = bf16[768,128]{1,0:T(8,128)(2,1)} fusion(bf16[1024,128]{1,0:T(8,128)(2,1)S(1)} %bitcast.105, s32[1024]{0:T(1024)S(1)} %pad_clamp_fusion.1), kind=kCustom, calls=%fused_computation.2 | custom fusion | bytes 396288 | tf_op jit(solution)/shard_map/gather | solution.py:114
  166.8 6.6 %all-to-all-start.4 = ((bf16[32,24,128]{2,1,0:T(8,128)(2,1)}), bf16[32,24,128]{2,1,0:T(8,128)(2,1)S(1)}, u32[]{:S(2)}, u32[]{:S(2)}) async-start(bf16[32,24,128]{2,1,0:T(8,128)(2,1)} %bitcast.13), calls=%async_computation.4 | async-start | bytes 393216 | tf_op jit(solution)/shard_map/all_to_all | solution.py:115
  173.5 8.3 %all-to-all-done.4 = bf16[32,24,128]{2,1,0:T(8,128)(2,1)S(1)} async-done(((bf16[32,24,128]{2,1,0:T(8,128)(2,1)}), bf16[32,24,128]{2,1,0:T(8,128)(2,1)S(1)}, u32[]{:S(2)}, u32[]{:S(2)}) %all-to-all-start.4) | async-done | bytes 196640 | tf_op jit(solution)/shard_map/all_to_all | solution.py:115
  181.8 1.3 gather_fusion.1
  (83 shorter events, 27.8 us)
Async XLA Ops:
  6.5 16.2 %copy-start = (bf16[128,128]{1,0:T(8,128)(2,1)S(1)}, bf16[128,128]{1,0:T(8,128)(2,1)}, u32[]{:S(2)}) copy-start(bf16[128,128]{1,0:T(8,128)(2,1)} %param.11) | copy-start | bytes 98308
  13.5 15.5 %all-to-all-start = ((s32[32,1,24]{2,1,0:T(1,128)}), s32[32,1,24]{2,1,0:T(1,128)S(1)}, u32[]{:S(2)}, u32[]{:S(2)}) async-start(s32[32,1,24]{2,1,0:T(1,128)} %bitcast.2), calls=%async_computation | async-start | bytes 32768 | tf_op jit(solution)/shard_map/all_to_all | solution.py:87
  28.9 13.2 %all-to-all-start.2 = ((bf16[32,24,128]{2,1,0:T(8,128)(2,1)}), bf16[32,24,128]{2,1,0:T(8,128)(2,1)S(1)}, u32[]{:S(2)}, u32[]{:S(2)}) async-start(bf16[32,24,128]{2,1,0:T(8,128)(2,1)} %bitcast.8), calls=%async_computation.2 | async-start | bytes 393216 | tf_op jit(solution)/shard_map/all_to_all | solution.py:86
  42.1 12.2 %all-to-all-start.1 = ((bf16[32,24,96]{2,1,0:T(8,128)(2,1)}), bf16[32,24,96]{2,1,0:T(8,128)(2,1)S(1)}, u32[]{:S(2)}, u32[]{:S(2)}) async-start(bf16[32,24,96]{2,1,0:T(8,128)(2,1)} %bitcast.3), calls=%async_computation.1 | async-start | bytes 393216 | tf_op jit(solution)/shard_map/all_to_all | solution.py:85
  56.2 13.8 %copy-start.3 = (u32[256]{0:T(256)S(1)}, u32[256]{0:T(256)}, u32[]{:S(2)}) copy-start(u32[256]{0:T(256)} %constant.52) | copy-start | bytes 3076
  56.2 15.0 %copy-start.1 = (s32[8]{0:T(128)S(1)}, s32[8]{0:T(128)}, u32[]{:S(2)}) copy-start(s32[8]{0:T(128)} %param.17) | copy-start | bytes 100
  56.2 78.8 %all-to-all-start.3 = ((bf16[8,8,128,128]{3,2,1,0:T(8,128)(2,1)}), bf16[8,8,128,128]{3,2,1,0:T(8,128)(2,1)S(1)}, u32[]{:S(2)}, u32[]{:S(2)}) async-start(bf16[8,8,128,128]{3,2,1,0:T(8,128)(2,1)} %stack.3), calls=%async_computation.3 | async-start | bytes 4194304 | tf_op jit(solution)/shard_map/all_to_all | solution.py:10
  64.5 70.5 %all-gather.2.cloned.1.call-start = ((), (), s32[]{:S(2)}) async-start(), calls=%async_computation.5 | async-start | bytes 1769472 | tf_op jit(solution)/shard_map/all_gather | solution.py:108
  164.2 18.9 %copy-start.2 = (s32[512]{0:T(512)S(1)}, s32[512]{0:T(512)}, u32[]{:S(2)}) copy-start(s32[512]{0:T(512)} %param.12) | copy-start | bytes 6148
  166.8 15.0 %all-to-all-start.4 = ((bf16[32,24,128]{2,1,0:T(8,128)(2,1)}), bf16[32,24,128]{2,1,0:T(8,128)(2,1)S(1)}, u32[]{:S(2)}, u32[]{:S(2)}) async-start(bf16[32,24,128]{2,1,0:T(8,128)(2,1)} %bitcast.13), calls=%async_computation.4 | async-start | bytes 393216 | tf_op jit(solution)/shard_map/all_to_all | solution.py:115
Sparse Core Ops, SparseCore 0:
  70.1 64.8 all-gather.1
